TPU v7x, 32 devices: a whole 2x2x4 slice. The times are simulated.
32 devices in a mesh: seg: 4 (over z), sec: 8 (over y, x, core).
Axes of the slice: x: 2, y: 2, z: 4, core: 2. Of those that a mesh axis runs over, the one named last changes fastest.
Arguments:
- start_vector: float32 [4, 1024, 2, 1024], P('seg', 'sec'), may hold values from -6 to 6
- left_env: bfloat16 [4, 5, 1024, 1024], P('seg', None, 'sec'), as said below
- right_env: bfloat16 [4, 5, 1024, 1024], P('seg', None, 'sec'), as said below
- charge_left: int32 [4, 1024], P('seg', 'sec'), may hold values from -8 to 8, as said below
- charge_right: int32 [4, 1024], P('seg'), may hold values from -8 to 8, as said below
Outputs:
- final_vector: float32 [4, 1024, 2, 1024], P('seg', 'sec')
- coefficients: float32 [4, 4], P('seg')
Inputs may be any that keep to these rules, and one draw needn't show every extreme that they name: `charge_left`: each segment's left bond holds both charges -8 and 8; charges gather near 0. `charge_right`: each segment's right bond holds both charges -8 and 8; charges gather near 0. left_env[g] is zero outside the charge rule stated for it, with the charges charge_left[(g + 1) mod 4]. right_env[g] is zero outside the charge rule stated for it, with the charges charge_right[(g - 1) mod 4].
All inputs are finite; a program needn't handle non-finite values.
Results may differ from a plain program's by a relative error of at most 0.0042.
Values may be sent and summed in bfloat16 or wider, within the bound.
A program may use at most 128 MiB of HBM per device.

v0:
```python
import jax
import jax.numpy as jnp
import numpy as np
from jax import lax
from jax.sharding import PartitionSpec as P

CHI = 1024
ITERS = 4


EPS = 1e-06


def shifted(value, axis, steps):
    count = lax.axis_size(axis)
    pairs = [(source, (source + steps) % count) for source in range(count)]
    return lax.ppermute(value, axis, pairs)


def mpo_table():
    identity = np.eye(2, dtype=np.float32)
    raising = np.array([[0.0, 0.0], [1.0, 0.0]], np.float32)
    lowering = np.array([[0.0, 1.0], [0.0, 0.0]], np.float32)
    diagonal_spin = np.array([[-0.5, 0.0], [0.0, 0.5]], np.float32)
    table = np.zeros((5, 5, 2, 2), np.float32)
    table[0, 0] = identity
    table[1, 0] = raising
    table[2, 0] = lowering
    table[3, 0] = diagonal_spin
    table[4, 1] = 0.5 * lowering
    table[4, 2] = 0.5 * raising
    table[4, 3] = diagonal_spin
    table[4, 4] = identity
    return table


def apply_operator(
    rounded_result, left_block_tensor, right_whole, operator_table, permitted_entries
):
    partial_left_contraction = jnp.einsum(
        "bkj,jet->bket",
        left_block_tensor,
        lax.all_gather(rounded_result, "sec", axis=0, tiled=True),
        preferred_element_type=jnp.float32,
    )
    mixed_terms = jnp.einsum(
        "abyx,alxr->blyr", operator_table, partial_left_contraction, precision=lax.Precision.HIGHEST
    )
    mixed_terms = mixed_terms.astype(jnp.bfloat16)
    operator_image = jnp.einsum(
        "blyr,brq->lyq", mixed_terms, right_whole, preferred_element_type=jnp.float32
    )
    return operator_image * permitted_entries


def on_device(start_vector, left_env, right_env, charge_left, charge_right):
    operator_table = jnp.asarray(mpo_table(), jnp.float32)
    left_block_tensor = shifted(left_env, "seg", 1)[0]
    passed = shifted(right_env, "seg", -1)
    right_whole = lax.all_gather(passed, "sec", axis=2, tiled=True)[0]
    spin_values = jnp.arange(2, dtype=jnp.int32)
    permitted_entries = (
        charge_right[0][None, None, :] == charge_left[0][:, None, None] + spin_values[None, :, None]
    ).astype(jnp.float32)
    current = start_vector[0] * permitted_entries
    norm_start = lax.psum(jnp.sum(current * current), "sec")
    current = current / jnp.sqrt(norm_start + EPS)
    previous = jnp.zeros_like(current)
    length_now = jnp.float32(0.0)
    lengths = []
    for iteration in range(ITERS):
        operator_image = apply_operator(
            current.astype(jnp.bfloat16),
            left_block_tensor,
            right_whole,
            operator_table,
            permitted_entries,
        )
        residual = operator_image - length_now * previous
        correlation = lax.psum(jnp.sum(residual * current), "sec")
        residual = residual - correlation * current
        length_now = jnp.sqrt(lax.psum(jnp.sum(residual * residual), "sec") + EPS)
        previous = current
        current = residual / length_now
        lengths.append(length_now)
    final_vector = (current * CHI)[None]
    coefficients = jnp.stack(lengths)[None]
    return (final_vector, coefficients)


def solution(mesh):
    return jax.shard_map(
        on_device,
        mesh=mesh,
        in_specs=(
            P("seg", "sec", None, None),
            P("seg", None, "sec", None),
            P("seg", None, "sec", None),
            P("seg", "sec"),
            P("seg", None),
        ),
        out_specs=(P("seg", "sec", None, None), P("seg", None)),
        check_vma=False,
    )
```

profile of v0, /device:TPU:0, one launch (start us, length us, event | category | flops | bytes accessed | tf_op | source)
XLA Modules:
  0.0 500.3 jit_solution(10242418832814374015)
XLA Ops:
  7.2 0.0 all-gather.6.cloned.1.call-start
  7.2 0.7 iota_add_fusion
  7.9 1.5 copy.12
  9.3 1.6 multiply_reduce_fusion.8
  11.0 15.8 %psum.63 = f32[]{:T(128)} all-reduce(f32[]{:T(128)} %multiply_reduce_fusion.8), channel_id=1, replica_groups=mesh['seg'=4,'sec'=8] {'sec'}, use_global_device_ids=true, to_apply=%region_1.0 | all-reduce | flops 1 | bytes 8 | tf_op jit(solution)/shard_map/psum | solution.py:66
  27.4 1.7 fusion.92
  29.1 0.0 all-gather.6.cloned.1.call-update
  29.2 0.0 all-gather.8.cloned.1.call-start
  29.2 3.7 collective-permute-start.1
  32.9 27.2 %collective-permute-done.1 = bf16[1,5,128,1024]{3,2,1,0:T(8,128)(2,1)S(1)} collective-permute-done((bf16[1,5,128,1024]{3,2,1,0:T(8,128)(2,1)}, bf16[1,5,128,1024]{3,2,1,0:T(8,128)(2,1)S(1)}, u32[]{:S(2)}, u32[]{:S(2)}) %collective-permute-start.1) | collective-permute-done | bytes 1310752 | tf_op jit(solution)/shard_map/ppermute | solution.py:17
  60.1 0.0 copy-start.2
  60.1 1.1 copy-done.2
  61.2 0.0 all-gather.8.cloned.1.call-update
  61.2 0.0 all-gather.10.cloned.1.call-start
  61.3 0.1 collective-permute-start
  61.4 29.7 %collective-permute-done = bf16[1,5,128,1024]{3,2,1,0:T(8,128)(2,1)S(1)} collective-permute-done((bf16[1,5,128,1024]{3,2,1,0:T(8,128)(2,1)}, bf16[1,5,128,1024]{3,2,1,0:T(8,128)(2,1)S(1)}, u32[]{:S(2)}, u32[]{:S(2)}) %collective-permute-start) | collective-permute-done | bytes 1310752 | tf_op jit(solution)/shard_map/ppermute | solution.py:17
  91.1 7.2 %fusion.24 = f32[5,128,2,1024,1]{1,3,0,2,4:T(8,128)} fusion(bf16[1024,2,1024]{0,2,1:T(8,128)(2,1)} %all-gather.6.cloned.1.call-done, bf16[1,5,128,1024]{3,2,1,0:T(8,128)(2,1)S(1)} %collective-permute-done), kind=kOutput, calls=%fused_computation.28 | convolution fusion | flops 2684354560 | bytes 10747904 | tf_op jit(solution)/shard_map/bkj,jet->bket/dot_general | solution.py:40
  98.3 0.0 copy-done.5
  98.3 8.4 %copy.27 = f32[5,128,2,1024,1]{3,0,2,4,1:T(8,128)} copy(f32[5,128,2,1024,1]{1,3,0,2,4:T(8,128)} %fusion.24) | data formatting | bytes 10485760 | tf_op jit(solution)/shard_map/bkj,jet->bket/dot_general | solution.py:40
  106.7 0.0 copy-done.3
  106.7 12.9 %fusion.8 = bf16[5,128,2,1024]{3,0,2,1:T(8,128)(2,1)} fusion(f32[5,128,2,1024,1]{3,0,2,4,1:T(8,128)} %copy.27, f32[5,5,2,2,1]{0,1,3,2,4:T(8,128)S(1)} %copy-done.3), kind=kOutput, calls=%fused_computation.12 | convolution fusion | flops 158597120 | bytes 7864720 | tf_op jit(solution)/shard_map/abyx,alxr->blyr/dot_general | solution.py:46
  119.5 11.6 %all-gather.8.cloned.1.call-done = bf16[1,5,1024,1024]{3,2,1,0:T(8,128)(2,1)} async-done(((bf16[1,5,128,1024]{3,2,1,0:T(8,128)(2,1)}), bf16[1,5,1024,1024]{3,2,1,0:T(8,128)(2,1)}) %all-gather.8.cloned.1.call-update) | async-done | bytes 10485776 | tf_op jit(solution)/shard_map/all_gather | solution.py:60
  131.1 0.0 copy-done.4
  131.1 11.8 %multiply_reduce_fusion.7 = (f32[]{:T(128)}, f32[128,2,1024]{0,2,1:T(8,128)S(1)}) fusion(f32[]{:T(128)S(6)} %sqrt.15, f32[1,128,2,1024]{1,3,2,0:T(8,128)S(1)} %copy.12, s32[128,2]{0,1:T(2,128)S(1)} %iota_add_fusion, s32[1024]{0:T(1024)S(1)} %bitcast.182, bf16[1,5,1024,1024]{3,2,1,0:T(8,128)(2,1)} %all-gather.8.cloned.1.call-done, ...), kind=kOutput, calls=%fused_computation.60 | convolution fusion | flops 2685927424 | bytes 15209480 | tf_op jit(solution)/shard_map/blyr,brq->lyq/dot_general | solution.py:50
  142.8 13.7 %psum.64 = f32[]{:T(128)} all-reduce(f32[]{:T(128)} %get-tuple-element.14), channel_id=1, replica_groups=mesh['seg'=4,'sec'=8] {'sec'}, use_global_device_ids=true, to_apply=%region_3.0 | all-reduce | flops 1 | bytes 8 | tf_op jit(solution)/shard_map/psum | solution.py:80
  156.5 1.6 multiply_reduce_fusion.6
  158.1 12.4 %psum.65 = f32[]{:T(128)} all-reduce(f32[]{:T(128)} %multiply_reduce_fusion.6), channel_id=1, replica_groups=mesh['seg'=4,'sec'=8] {'sec'}, use_global_device_ids=true, to_apply=%region_5.0 | all-reduce | flops 1 | bytes 8 | tf_op jit(solution)/shard_map/psum | solution.py:82
  171.2 1.8 fusion.95
  173.0 0.0 all-gather.10.cloned.1.call-update
  173.0 0.2 all-gather.12.cloned.1.call-start
  173.3 37.3 %all-gather.10.cloned.1.call-done = bf16[1024,2,1024]{0,2,1:T(8,128)(2,1)} async-done(((bf16[128,2,1024]{0,2,1:T(8,128)(2,1)}), bf16[1024,2,1024]{0,2,1:T(8,128)(2,1)}) %all-gather.10.cloned.1.call-update) | async-done | bytes 4194320 | tf_op jit(solution)/shard_map/all_gather | solution.py:43
  210.6 7.1 %fusion.27 = f32[5,128,2,1024,1]{1,3,0,2,4:T(8,128)} fusion(bf16[1024,2,1024]{0,2,1:T(8,128)(2,1)} %all-gather.10.cloned.1.call-done, bf16[1,5,128,1024]{3,2,1,0:T(8,128)(2,1)} %copy-done.5), kind=kOutput, calls=%fused_computation.29 | convolution fusion | flops 2684354560 | bytes 10747904 | tf_op jit(solution)/shard_map/bkj,jet->bket/dot_general | solution.py:40
  217.7 8.0 %copy.31 = f32[5,128,2,1024,1]{3,0,2,4,1:T(8,128)} copy(f32[5,128,2,1024,1]{1,3,0,2,4:T(8,128)} %fusion.27) | data formatting | bytes 10485760 | tf_op jit(solution)/shard_map/bkj,jet->bket/dot_general | solution.py:40
  225.7 11.7 %fusion.9 = bf16[5,128,2,1024]{3,0,2,1:T(8,128)(2,1)S(1)} fusion(f32[5,128,2,1024,1]{3,0,2,4,1:T(8,128)} %copy.31, f32[5,5,2,2,1]{0,1,3,2,4:T(8,128)S(1)} %copy-done.3), kind=kOutput, calls=%fused_computation.13 | convolution fusion | flops 158597120 | bytes 7864720 | tf_op jit(solution)/shard_map/abyx,alxr->blyr/dot_general | solution.py:46
  237.4 11.1 %multiply_reduce_fusion.5 = (f32[]{:T(128)}, f32[128,2,1024]{0,2,1:T(8,128)S(1)}) fusion(f32[128,2,1024]{0,2,1:T(8,128)S(1)} %get-tuple-element.13, f32[]{:T(128)S(6)} %sqrt.15, f32[1,128,2,1024]{1,3,2,0:T(8,128)S(1)} %copy.12, f32[]{:T(128)} %sqrt.16, bf16[1,5,1024,1024]{3,2,1,0:T(8,128)(2,1)} %all-gather.8.cloned.1.call-done, ...), kind=kOutput, calls=%fused_computation.57 | convolution fusion | flops 2686451712 | bytes 16258060 | tf_op jit(solution)/shard_map/blyr,brq->lyq/dot_general | solution.py:50
  248.5 13.7 %psum.66 = f32[]{:T(128)} all-reduce(f32[]{:T(128)} %get-tuple-element.16), channel_id=1, replica_groups=mesh['seg'=4,'sec'=8] {'sec'}, use_global_device_ids=true, to_apply=%region_7.0 | all-reduce | flops 1 | bytes 8 | tf_op jit(solution)/shard_map/psum | solution.py:80
  262.2 1.6 multiply_reduce_fusion.4
  263.8 12.5 %psum.67 = f32[]{:T(128)} all-reduce(f32[]{:T(128)} %multiply_reduce_fusion.4), channel_id=1, replica_groups=mesh['seg'=4,'sec'=8] {'sec'}, use_global_device_ids=true, to_apply=%region_9.0 | all-reduce | flops 1 | bytes 8 | tf_op jit(solution)/shard_map/psum | solution.py:82
  276.9 0.0 copy-done
  277.0 2.9 fusion.94
  279.8 0.0 all-gather.12.cloned.1.call-update
  279.9 0.3 all-gather.14.cloned.1.call-start
  280.1 37.3 %all-gather.12.cloned.1.call-done = bf16[1024,2,1024]{0,2,1:T(8,128)(2,1)} async-done(((bf16[128,2,1024]{0,2,1:T(8,128)(2,1)}), bf16[1024,2,1024]{0,2,1:T(8,128)(2,1)}) %all-gather.12.cloned.1.call-update) | async-done | bytes 4194320 | tf_op jit(solution)/shard_map/all_gather | solution.py:43
  317.4 7.1 %fusion.30 = f32[5,128,2,1024,1]{1,3,0,2,4:T(8,128)} fusion(bf16[1024,2,1024]{0,2,1:T(8,128)(2,1)} %all-gather.12.cloned.1.call-done, bf16[1,5,128,1024]{3,2,1,0:T(8,128)(2,1)} %copy-done.5), kind=kOutput, calls=%fused_computation.30 | convolution fusion | flops 2684354560 | bytes 10747904 | tf_op jit(solution)/shard_map/bkj,jet->bket/dot_general | solution.py:40
  324.5 8.0 %copy.35 = f32[5,128,2,1024,1]{3,0,2,4,1:T(8,128)} copy(f32[5,128,2,1024,1]{1,3,0,2,4:T(8,128)} %fusion.30) | data formatting | bytes 10485760 | tf_op jit(solution)/shard_map/bkj,jet->bket/dot_general | solution.py:40
  332.5 11.7 %fusion.10 = bf16[5,128,2,1024]{3,0,2,1:T(8,128)(2,1)S(1)} fusion(f32[5,128,2,1024,1]{3,0,2,4,1:T(8,128)} %copy.35, f32[5,5,2,2,1]{0,1,3,2,4:T(8,128)S(1)} %copy-done.3), kind=kOutput, calls=%fused_computation.14 | convolution fusion | flops 158597120 | bytes 7864720 | tf_op jit(solution)/shard_map/abyx,alxr->blyr/dot_general | solution.py:46
  344.2 11.1 %multiply_reduce_fusion.3 = (f32[]{:T(128)}, f32[128,2,1024]{0,2,1:T(8,128)S(1)}) fusion(f32[128,2,1024]{0,2,1:T(8,128)S(1)} %get-tuple-element.11, f32[128,2,1024]{0,2,1:T(8,128)S(1)} %get-tuple-element.13, f32[]{:T(128)} %sqrt.17, bf16[1,5,1024,1024]{3,2,1,0:T(8,128)(2,1)} %all-gather.8.cloned.1.call-done, bf16[5,128,2,1024]{3,0,2,1:T(8,128)(2,1)S(1)} %fusion.10, ...), kind=kOutput, calls=%fused_computation.54 | convolution fusion | flops 2685927424 | bytes 16258056 | tf_op jit(solution)/shard_map/blyr,brq->lyq/dot_general | solution.py:50
  355.3 13.7 %psum.68 = f32[]{:T(128)} all-reduce(f32[]{:T(128)} %get-tuple-element.18), channel_id=1, replica_groups=mesh['seg'=4,'sec'=8] {'sec'}, use_global_device_ids=true, to_apply=%region_11.0 | all-reduce | flops 1 | bytes 8 | tf_op jit(solution)/shard_map/psum | solution.py:80
  369.0 1.6 multiply_reduce_fusion.2
  370.6 12.7 %psum.69 = f32[]{:T(128)} all-reduce(f32[]{:T(128)} %multiply_reduce_fusion.2), channel_id=1, replica_groups=mesh['seg'=4,'sec'=8] {'sec'}, use_global_device_ids=true, to_apply=%region_13.0 | all-reduce | flops 1 | bytes 8 | tf_op jit(solution)/shard_map/psum | solution.py:82
  384.0 0.0 copy-done.1
  384.0 2.9 fusion.93
  386.9 0.0 all-gather.14.cloned.1.call-update
  386.9 37.5 %all-gather.14.cloned.1.call-done = bf16[1024,2,1024]{0,2,1:T(8,128)(2,1)} async-done(((bf16[128,2,1024]{0,2,1:T(8,128)(2,1)}), bf16[1024,2,1024]{0,2,1:T(8,128)(2,1)}) %all-gather.14.cloned.1.call-update) | async-done | bytes 4194320 | tf_op jit(solution)/shard_map/all_gather | solution.py:43
  424.4 7.1 %fusion.33 = f32[5,128,2,1024,1]{1,3,0,2,4:T(8,128)} fusion(bf16[1024,2,1024]{0,2,1:T(8,128)(2,1)} %all-gather.14.cloned.1.call-done, bf16[1,5,128,1024]{3,2,1,0:T(8,128)(2,1)} %copy-done.5), kind=kOutput, calls=%fused_computation.31 | convolution fusion | flops 2684354560 | bytes 10747904 | tf_op jit(solution)/shard_map/bkj,jet->bket/dot_general | solution.py:40
  431.5 8.0 %copy.39 = f32[5,128,2,1024,1]{3,0,2,4,1:T(8,128)} copy(f32[5,128,2,1024,1]{1,3,0,2,4:T(8,128)} %fusion.33) | data formatting | bytes 10485760 | tf_op jit(solution)/shard_map/bkj,jet->bket/dot_general | solution.py:40
  439.5 11.7 %fusion.11 = bf16[5,128,2,1024]{3,0,2,1:T(8,128)(2,1)S(1)} fusion(f32[5,128,2,1024,1]{3,0,2,4,1:T(8,128)} %copy.39, f32[5,5,2,2,1]{0,1,3,2,4:T(8,128)S(1)} %copy-done.3), kind=kOutput, calls=%fused_computation.15 | convolution fusion | flops 158597120 | bytes 7864720 | tf_op jit(solution)/shard_map/abyx,alxr->blyr/dot_general | solution.py:46
  451.3 11.1 %multiply_reduce_fusion.1 = (f32[]{:T(128)}, f32[128,2,1024]{0,2,1:T(8,128)S(1)}) fusion(f32[128,2,1024]{0,2,1:T(8,128)S(1)} %get-tuple-element.9, f32[128,2,1024]{0,2,1:T(8,128)S(1)} %get-tuple-element.11, f32[]{:T(128)} %sqrt.18, bf16[1,5,1024,1024]{3,2,1,0:T(8,128)(2,1)} %all-gather.8.cloned.1.call-done, bf16[5,128,2,1024]{3,0,2,1:T(8,128)(2,1)S(1)} %fusion.11, ...), kind=kOutput, calls=%fused_computation.51 | convolution fusion | flops 2685927424 | bytes 16258056 | tf_op jit(solution)/shard_map/blyr,brq->lyq/dot_general | solution.py:50
  462.3 13.7 %psum.70 = f32[]{:T(128)} all-reduce(f32[]{:T(128)} %get-tuple-element.20), channel_id=1, replica_groups=mesh['seg'=4,'sec'=8] {'sec'}, use_global_device_ids=true, to_apply=%region_15.0 | all-reduce | flops 1 | bytes 8 | tf_op jit(solution)/shard_map/psum | solution.py:80
  476.1 1.5 multiply_reduce_fusion
  477.6 12.4 %psum.71 = f32[]{:T(128)} all-reduce(f32[]{:T(128)} %multiply_reduce_fusion), channel_id=1, replica_groups=mesh['seg'=4,'sec'=8] {'sec'}, use_global_device_ids=true, to_apply=%region_17.0 | all-reduce | flops 1 | bytes 8 | tf_op jit(solution)/shard_map/psum | solution.py:82
  490.7 0.8 multiply_bitcast_fusion
  491.5 1.3 copy.25
  492.8 0.6 maximum_bitcast_fusion
  (6 shorter events, 0.0 us)
Async XLA Ops:
  7.2 83.9 %all-gather.6.cloned.1.call-start = ((), (), s32[]{:S(2)}) async-start(), calls=%async_computation | async-start | bytes 4718592 | tf_op jit(solution)/shard_map/all_gather | solution.py:43
  29.2 101.9 %all-gather.8.cloned.1.call-start = ((), (), s32[]{:S(2)}) async-start(), calls=%async_computation.1 | async-start | bytes 11796480 | tf_op jit(solution)/shard_map/all_gather | solution.py:60
  29.2 30.9 %collective-permute-start.1 = (bf16[1,5,128,1024]{3,2,1,0:T(8,128)(2,1)}, bf16[1,5,128,1024]{3,2,1,0:T(8,128)(2,1)S(1)}, u32[]{:S(2)}, u32[]{:S(2)}) collective-permute-start(bf16[1,5,128,1024]{3,2,1,0:T(8,128)(2,1)} %param.8), channel_id=1, source_target_pairs={{0,24},{8,0},{16,8},{24,16},{1,25},{9,1},{17,9},{25,17},{2,26},{10... | collective-permute-start | bytes 3932168 | tf_op jit(solution)/shard_map/ppermute | solution.py:17
  60.1 1.1 copy-start.2
  61.2 149.3 %all-gather.10.cloned.1.call-start = ((), (), s32[]{:S(2)}) async-start(), calls=%async_computation.2 | async-start | bytes 4718592 | tf_op jit(solution)/shard_map/all_gather | solution.py:43
  61.3 29.8 %collective-permute-start = (bf16[1,5,128,1024]{3,2,1,0:T(8,128)(2,1)}, bf16[1,5,128,1024]{3,2,1,0:T(8,128)(2,1)S(1)}, u32[]{:S(2)}, u32[]{:S(2)}) collective-permute-start(bf16[1,5,128,1024]{3,2,1,0:T(8,128)(2,1)} %param.7), channel_id=1, source_target_pairs={{0,8},{8,16},{16,24},{24,0},{1,9},{9,17},{17,25},{25,1},{2,10},{10... | collective-permute-start | bytes 3932168 | tf_op jit(solution)/shard_map/ppermute | solution.py:17
  91.1 7.2 %copy-start.5 = (bf16[1,5,128,1024]{3,2,1,0:T(8,128)(2,1)}, bf16[1,5,128,1024]{3,2,1,0:T(8,128)(2,1)S(1)}, u32[]{:S(2)}) copy-start(bf16[1,5,128,1024]{3,2,1,0:T(8,128)(2,1)S(1)} %collective-permute-done) | copy-start | bytes 3932164
  98.3 8.4 %copy-start.3 = (f32[5,5,2,2,1]{0,1,3,2,4:T(8,128)S(1)}, f32[5,5,2,2,1]{0,1,3,2,4:T(8,128)}, u32[]{:S(2)}) copy-start(f32[5,5,2,2,1]{0,1,3,2,4:T(8,128)} %constant.19) | copy-start | bytes 1204
  106.7 24.4 %copy-start.4 = (s32[1,1024]{1,0:T(1,128)S(1)}, s32[1,1024]{1,0:T(1,128)}, u32[]{:S(2)}) copy-start(s32[1,1024]{1,0:T(1,128)} %param.10) | copy-start | bytes 12292
  173.0 144.3 %all-gather.12.cloned.1.call-start = ((), (), s32[]{:S(2)}) async-start(), calls=%async_computation.3 | async-start | bytes 4718592 | tf_op jit(solution)/shard_map/all_gather | solution.py:43
  248.5 28.4 %copy-start = (f32[128,2,1024]{0,2,1:T(8,128)}, f32[128,2,1024]{0,2,1:T(8,128)S(1)}, u32[]{:S(2)}) copy-start(f32[128,2,1024]{0,2,1:T(8,128)S(1)} %get-tuple-element.17) | copy-start | bytes 3145732
  279.9 144.6 %all-gather.14.cloned.1.call-start = ((), (), s32[]{:S(2)}) async-start(), calls=%async_computation.4 | async-start | bytes 4718592 | tf_op jit(solution)/shard_map/all_gather | solution.py:43
  355.3 28.7 %copy-start.1 = (f32[128,2,1024]{0,2,1:T(8,128)}, f32[128,2,1024]{0,2,1:T(8,128)S(1)}, u32[]{:S(2)}) copy-start(f32[128,2,1024]{0,2,1:T(8,128)S(1)} %get-tuple-element.19) | copy-start | bytes 3145732
Sparse Core Ops, SparseCore 0:
  29.3 36.6 all-gather.5
  67.9 63.1 all-gather.7
  173.2 37.3 all-gather.9
  280.0 37.3 all-gather.11
  387.0 37.3 all-gather.13
where the time goes:
time: 509 us; the launch traced here: 500 us
  waiting for transfers between devices  181 us (36%)
  matrix products  122 us (24%)
  blocking collectives  121 us (24%)
  local copies, waits for them, and re-layouts  36.3 us (7%)
  other arithmetic  19.1 us (4%)
  between operations  17.8 us (3%)
    all_gather x4, waiting for transfers between devices, apply_operator(): lax.all_gather(rounded_result, 'sec', axis=0, tiled=True)  112 us
    ppermute x2, waiting for transfers between devices, shifted(): return lax.ppermute(value, axis, pairs)  56.9 us
    psum x4, blocking collectives, on_device(): correlation = lax.psum(jnp.sum(residual * current), 'sec')  54.8 us
    psum x4, blocking collectives, on_device(): length_now = jnp.sqrt(lax.psum(jnp.sum(residual * residual), 'sec') + EPS)  50 us
    dot_general x4, matrix products, apply_operator(): jnp.einsum('abyx,alxr->blyr', operator_table, partial_left_contraction, p...  48.1 us
    dot_general x4, matrix products, apply_operator(): jnp.einsum('blyr,brq->lyq', mixed_terms, right_whole, preferred_element_t...  44.9 us
    dot_general x4, local copies, waits for them, and re-layouts, apply_operator(): jnp.einsum('bkj,jet->bket', left_block_tensor, lax.all_gather(rounded_res...  32.4 us
    dot_general x4, matrix products, apply_operator(): jnp.einsum('bkj,jet->bket', left_block_tensor, lax.all_gather(rounded_res...  28.6 us
  transfers between devices with their start and end apart: 7, of which 6 were waited for; matrix products, arithmetic and copies ran while one was open for 6% of the time, Pallas kernels for 0%

commit v1 on v0

v1 whole, which is shorter than its diff:
```python
import jax
import jax.numpy as jnp
from jax import lax
from jax.sharding import PartitionSpec as P

CHI = 1024
ITERS = 4


EPS = 1e-06


def shifted(value, axis, steps):
    count = lax.axis_size(axis)
    pairs = [(source, (source + steps) % count) for source in range(count)]
    return lax.ppermute(value, axis, pairs)


def merged(env):
    return jnp.stack([env[0] + env[1] + env[2], env[3], env[4]])


def on_device(start_vector, left_env, right_env, charge_left, charge_right):
    left = shifted(merged(left_env[0]), "seg", 1)
    passed = shifted(merged(right_env[0]), "seg", -1)
    right = lax.all_gather(passed, "sec", axis=1, tiled=True)
    charges = charge_right[0]
    step = charges[None, :] - charges[:, None]
    right_stack = jnp.concatenate(
        [
            jnp.where(step == 0, right[0], 0),
            jnp.where(step == 1, right[0], 0),
            jnp.where(step == -1, right[0], 0),
            right[1],
            right[2],
        ],
        axis=0,
    )
    gap = charges[None, :] - charge_left[0][:, None]
    down, up = gap == 0, gap == 1
    allowed = down | up
    spin = jnp.where(up, 0.5, -0.5)
    rows = gap.shape[0]
    left_rows = left.reshape(3 * rows, left.shape[2])

    current = jnp.where(down, start_vector[0, :, 0], jnp.where(up, start_vector[0, :, 1], 0.0))
    norm = lax.psum(jnp.sum(current * current), "sec")
    current = current / jnp.sqrt(norm + EPS)
    previous = jnp.zeros_like(current)
    beta = jnp.float32(0.0)
    betas = []
    for _ in range(ITERS):
        whole = lax.all_gather(current.astype(jnp.bfloat16), "sec", axis=0, tiled=True)
        first = jnp.dot(left_rows, whole, preferred_element_type=jnp.float32)
        first = first.reshape(3, rows, -1)
        half = 0.5 * first[2]
        mixed = jnp.concatenate(
            [
                jnp.where(allowed, first[0] + spin * first[1], 0.0),
                jnp.where(up, half, 0.0),
                jnp.where(down, half, 0.0),
                jnp.where(allowed, spin * first[2], 0.0),
                jnp.where(allowed, first[2], 0.0),
            ],
            axis=1,
        ).astype(jnp.bfloat16)
        image = jnp.dot(mixed, right_stack, preferred_element_type=jnp.float32)
        residual = jnp.where(allowed, image, 0.0) - beta * previous
        alpha = lax.psum(jnp.sum(residual * current), "sec")
        residual = residual - alpha * current
        beta = jnp.sqrt(lax.psum(jnp.sum(residual * residual), "sec") + EPS)
        previous = current
        current = residual / beta
        betas.append(beta)
    scaled = current * CHI
    final = jnp.stack([jnp.where(down, scaled, 0.0), jnp.where(up, scaled, 0.0)], axis=1)
    return final[None], jnp.stack(betas)[None]


def solution(mesh):
    return jax.shard_map(
        on_device,
        mesh=mesh,
        in_specs=(
            P("seg", "sec", None, None),
            P("seg", None, "sec", None),
            P("seg", None, "sec", None),
            P("seg", "sec"),
            P("seg", None),
        ),
        out_specs=(P("seg", "sec", None, None), P("seg", None)),
        check_vma=False,
    )
```

time: 509 us -> 354 us (0.70); the launches traced: 500 us -> 353 us
  matrix products: 122 us -> 32.1 us
  waiting for transfers between devices: 181 us -> 150 us
  local copies, waits for them, and re-layouts: 36.3 us -> 6.75 us
    dot_general x12 -> x8, matrix products: 122 us -> 32.1 us  [the longest x4 21.8 us: on_device(): image = jnp.dot(mixed, right_stack, preferred_element_type=jnp.float32)]
    dot_general x4 -> x0, local copies, waits for them, and re-layouts: 32.4 us -> none  [apply_operator(): jnp.einsum('bkj,jet->bket', left_block_tensor, lax.all_gather(rounded_res...]
    ppermute x2, waiting for transfers between devices: 56.9 us -> 34.1 us  [shifted(): return lax.ppermute(value, axis, pairs)]
    unnamed x0 -> x19, other arithmetic: none -> 8.02 us
    all_gather x5, waiting for transfers between devices: 124 us -> 116 us  [the longest x4 83.5 us: on_device(): lax.all_gather(current.astype(jnp.bfloat16), 'sec', axis=0, tiled=True)]
  transfers between devices with their start and end apart: 7 -> 7, of which waited for: 6 -> 6; matrix products, arithmetic and copies ran while one was open for 6% -> 1% of each run, Pallas kernels for 0% -> 0%
where the time goes in v1:
time: 354 us; the launch traced here: 353 us
  waiting for transfers between devices  150 us (42%)
  blocking collectives  120 us (34%)
  matrix products  32.1 us (9%)
  other arithmetic  22.3 us (6%)
  between operations  17.6 us (5%)
  local copies, waits for them, and re-layouts  6.75 us (2%)
  starting transfers between devices  4.1 us (1%)
    all_gather x4, waiting for transfers between devices, on_device(): lax.all_gather(current.astype(jnp.bfloat16), 'sec', axis=0, tiled=True)  83.5 us
    psum x4, blocking collectives, on_device(): alpha = lax.psum(jnp.sum(residual * current), 'sec')  54.8 us
    psum x4, blocking collectives, on_device(): beta = jnp.sqrt(lax.psum(jnp.sum(residual * residual), 'sec') + EPS)  49.6 us
    ppermute x2, waiting for transfers between devices, shifted(): return lax.ppermute(value, axis, pairs)  34.1 us
    all_gather x1, waiting for transfers between devices, on_device(): right = lax.all_gather(passed, 'sec', axis=1, tiled=True)  32.6 us
    dot_general x4, matrix products, on_device(): image = jnp.dot(mixed, right_stack, preferred_element_type=jnp.float32)  21.8 us
    psum x1, blocking collectives, on_device(): norm = lax.psum(jnp.sum(current * current), 'sec')  15.8 us
    dot_general x4, matrix products, on_device(): first = jnp.dot(left_rows, whole, preferred_element_type=jnp.float32)  10.3 us
  transfers between devices with their start and end apart: 7, of which 6 were waited for; matrix products, arithmetic and copies ran while one was open for 1% of the time, Pallas kernels for 0%

profile of v1, /device:TPU:0, one launch (start us, length us, event | category | flops | bytes accessed | tf_op | source)
XLA Modules:
  0.0 353.4 jit_solution(2616346199038595305)
XLA Ops:
  7.2 2.5 fusion.78
  9.8 1.0 multiply_reduce_fusion.8
  10.7 15.8 %psum.63 = f32[]{:T(128)} all-reduce(f32[]{:T(128)} %multiply_reduce_fusion.8), channel_id=1, replica_groups=mesh['seg'=4,'sec'=8] {'sec'}, use_global_device_ids=true, to_apply=%region_1.2 | all-reduce | flops 1 | bytes 8 | tf_op jit(solution)/shard_map/psum | solution.py:47
  27.2 1.0 fusion.77
  28.5 3.7 %collective-permute-start.1 = (bf16[3,128,1024]{2,1,0:T(8,128)(2,1)S(1)}, bf16[3,128,1024]{2,1,0:T(8,128)(2,1)S(1)}, u32[]{:S(2)}, u32[]{:S(2)}) collective-permute-start(bf16[3,128,1024]{2,1,0:T(8,128)(2,1)S(1)} %pad_maximum_fusion.1), channel_id=1, source_target_pairs={{0,24},{8,0},{16,8},{24,16},{1,25},{9,1},{17,9},{25,17},{2,26},{10... | collective-permute-start | bytes 2359304 | tf_op jit(solution)/shard_map/ppermute | solution.py:16
  32.1 16.1 %collective-permute-done.1 = bf16[3,128,1024]{2,1,0:T(8,128)(2,1)S(1)} collective-permute-done((bf16[3,128,1024]{2,1,0:T(8,128)(2,1)S(1)}, bf16[3,128,1024]{2,1,0:T(8,128)(2,1)S(1)}, u32[]{:S(2)}, u32[]{:S(2)}) %collective-permute-start.1) | collective-permute-done | bytes 786464 | tf_op jit(solution)/shard_map/ppermute | solution.py:16
  48.2 0.9 copy-done.5
  49.4 18.0 %collective-permute-done = bf16[3,128,1024]{2,1,0:T(8,128)(2,1)S(1)} collective-permute-done((bf16[3,128,1024]{2,1,0:T(8,128)(2,1)S(1)}, bf16[3,128,1024]{2,1,0:T(8,128)(2,1)S(1)}, u32[]{:S(2)}, u32[]{:S(2)}) %collective-permute-start) | collective-permute-done | bytes 786464 | tf_op jit(solution)/shard_map/ppermute | solution.py:16
  67.4 2.6 fusion.79
  70.0 0.2 fusion.65
  70.2 0.1 fusion.69
  70.3 0.1 fusion.73
  70.5 0.2 fusion.64
  70.7 0.1 fusion.54
  70.8 32.6 %all-gather.8.cloned.1.call-done = bf16[3,1024,1024]{2,1,0:T(8,128)(2,1)} async-done(((bf16[3,128,1024]{2,1,0:T(8,128)(2,1)}), bf16[3,1024,1024]{2,1,0:T(8,128)(2,1)}) %all-gather.8.cloned.1.call-update) | async-done | bytes 6291472 | tf_op jit(solution)/shard_map/all_gather | solution.py:26
  103.4 2.4 fusion.5
  105.8 2.3 fusion.4
  108.1 0.7 fusion.3
  108.8 0.2 fusion.7
  109.0 0.2 fusion.6
  109.2 2.8 multiply_reduce_fusion.7
  112.0 1.2 copy-done
  113.2 13.7 %psum.64 = f32[]{:T(128)} all-reduce(f32[]{:T(128)} %get-tuple-element.22), channel_id=1, replica_groups=mesh['seg'=4,'sec'=8] {'sec'}, use_global_device_ids=true, to_apply=%region_3.4 | all-reduce | flops 1 | bytes 8 | tf_op jit(solution)/shard_map/psum | solution.py:69
  126.9 1.4 multiply_reduce_fusion.6
  128.3 12.4 %psum.65 = f32[]{:T(128)} all-reduce(f32[]{:T(128)} %multiply_reduce_fusion.6), channel_id=1, replica_groups=mesh['seg'=4,'sec'=8] {'sec'}, use_global_device_ids=true, to_apply=%region_5.6 | all-reduce | flops 1 | bytes 8 | tf_op jit(solution)/shard_map/psum | solution.py:71
  141.4 1.5 fusion.76
  142.9 27.9 %all-gather.10.cloned.1.call-done = bf16[1024,1024]{1,0:T(8,128)(2,1)} async-done(((bf16[128,1024]{1,0:T(8,128)(2,1)}), bf16[1024,1024]{1,0:T(8,128)(2,1)}) %all-gather.10.cloned.1.call-update) | async-done | bytes 2097168 | tf_op jit(solution)/shard_map/all_gather | solution.py:53
  170.8 2.6 fusion.80
  173.4 0.2 fusion.63
  173.6 0.1 fusion.68
  173.7 0.1 fusion.72
  173.9 0.2 fusion.62
  174.1 0.1 fusion.55
  174.2 6.3 %multiply_reduce_fusion.5 = (f32[]{:T(128)}, f32[128,1024]{1,0:T(8,128)S(1)}) fusion(f32[128,1024]{1,0:T(8,128)S(1)} %get-tuple-element.9, f32[128,1024]{1,0:T(8,128)S(1)} %get-tuple-element.11, f32[]{:T(128)} %sqrt.16, bf16[128,5120]{1,0:T(8,128)(2,1)S(1)} %fusion.55, bf16[5120,1024]{1,0:T(8,128)(2,1)} %copy-done, s32[128]{0:T(128)S(1)} %bitcast.120, ...), kind=kOutput, calls=%fused_computation.90 | convolution fusion | flops 1343356928 | bytes 13373960 | tf_op jit(solution)/shard_map/dot_general | solution.py:67
  180.6 13.7 %psum.66 = f32[]{:T(128)} all-reduce(f32[]{:T(128)} %get-tuple-element.24), channel_id=1, replica_groups=mesh['seg'=4,'sec'=8] {'sec'}, use_global_device_ids=true, to_apply=%region_7.8 | all-reduce | flops 1 | bytes 8 | tf_op jit(solution)/shard_map/psum | solution.py:69
  194.3 1.4 multiply_reduce_fusion.4
  195.7 12.4 %psum.67 = f32[]{:T(128)} all-reduce(f32[]{:T(128)} %multiply_reduce_fusion.4), channel_id=1, replica_groups=mesh['seg'=4,'sec'=8] {'sec'}, use_global_device_ids=true, to_apply=%region_9.10 | all-reduce | flops 1 | bytes 8 | tf_op jit(solution)/shard_map/psum | solution.py:71
  208.8 1.5 fusion.75
  210.3 0.2 all-gather.14.cloned.1.call-start
  210.5 27.7 %all-gather.12.cloned.1.call-done = bf16[1024,1024]{1,0:T(8,128)(2,1)} async-done(((bf16[128,1024]{1,0:T(8,128)(2,1)}), bf16[1024,1024]{1,0:T(8,128)(2,1)}) %all-gather.12.cloned.1.call-update) | async-done | bytes 2097168 | tf_op jit(solution)/shard_map/all_gather | solution.py:53
  238.2 2.6 fusion.81
  240.8 0.2 fusion.61
  241.0 0.1 fusion.67
  241.1 0.1 fusion.71
  241.3 0.2 fusion.60
  241.5 0.1 fusion.56
  241.6 6.3 %multiply_reduce_fusion.3 = (f32[]{:T(128)}, f32[128,1024]{1,0:T(8,128)S(1)}) fusion(f32[128,1024]{1,0:T(8,128)S(1)} %get-tuple-element.7, f32[128,1024]{1,0:T(8,128)S(1)} %get-tuple-element.9, f32[]{:T(128)} %sqrt.17, bf16[128,5120]{1,0:T(8,128)(2,1)S(1)} %fusion.56, bf16[5120,1024]{1,0:T(8,128)(2,1)} %copy-done, s32[128]{0:T(128)S(1)} %bitcast.126, ...), kind=kOutput, calls=%fused_computation.86 | convolution fusion | flops 1343356928 | bytes 13373960 | tf_op jit(solution)/shard_map/dot_general | solution.py:67
  248.0 13.7 %psum.68 = f32[]{:T(128)} all-reduce(f32[]{:T(128)} %get-tuple-element.26), channel_id=1, replica_groups=mesh['seg'=4,'sec'=8] {'sec'}, use_global_device_ids=true, to_apply=%region_11.12 | all-reduce | flops 1 | bytes 8 | tf_op jit(solution)/shard_map/psum | solution.py:69
  261.7 1.4 multiply_reduce_fusion.2
  263.1 12.4 %psum.69 = f32[]{:T(128)} all-reduce(f32[]{:T(128)} %multiply_reduce_fusion.2), channel_id=1, replica_groups=mesh['seg'=4,'sec'=8] {'sec'}, use_global_device_ids=true, to_apply=%region_13.14 | all-reduce | flops 1 | bytes 8 | tf_op jit(solution)/shard_map/psum | solution.py:71
  276.2 1.5 fusion.74
  277.6 27.9 %all-gather.14.cloned.1.call-done = bf16[1024,1024]{1,0:T(8,128)(2,1)} async-done(((bf16[128,1024]{1,0:T(8,128)(2,1)}), bf16[1024,1024]{1,0:T(8,128)(2,1)}) %all-gather.14.cloned.1.call-update) | async-done | bytes 2097168 | tf_op jit(solution)/shard_map/all_gather | solution.py:53
  305.6 2.6 fusion.82
  308.2 0.2 fusion.59
  308.5 0.1 fusion.70
  308.7 0.2 fusion.58
  308.9 0.1 fusion.57
  309.0 6.3 %multiply_reduce_fusion.1 = (f32[]{:T(128)}, f32[128,1024]{1,0:T(8,128)S(1)}) fusion(f32[128,1024]{1,0:T(8,128)S(1)} %get-tuple-element.5, f32[128,1024]{1,0:T(8,128)S(1)} %get-tuple-element.7, f32[]{:T(128)} %sqrt.18, bf16[128,5120]{1,0:T(8,128)(2,1)S(1)} %fusion.57, bf16[5120,1024]{1,0:T(8,128)(2,1)} %copy-done, s32[128]{0:T(128)S(1)} %bitcast.132, ...), kind=kOutput, calls=%fused_computation.82 | convolution fusion | flops 1343356928 | bytes 13373960 | tf_op jit(solution)/shard_map/dot_general | solution.py:67
  315.4 13.7 %psum.70 = f32[]{:T(128)} all-reduce(f32[]{:T(128)} %get-tuple-element.28), channel_id=1, replica_groups=mesh['seg'=4,'sec'=8] {'sec'}, use_global_device_ids=true, to_apply=%region_15.16 | all-reduce | flops 1 | bytes 8 | tf_op jit(solution)/shard_map/psum | solution.py:69
  329.1 1.4 multiply_reduce_fusion
  330.4 12.4 %psum.71 = f32[]{:T(128)} all-reduce(f32[]{:T(128)} %multiply_reduce_fusion), channel_id=1, replica_groups=mesh['seg'=4,'sec'=8] {'sec'}, use_global_device_ids=true, to_apply=%region_17.18 | all-reduce | flops 1 | bytes 8 | tf_op jit(solution)/shard_map/psum | solution.py:71
  343.5 0.8 fusion.28
  344.5 1.8 copy.9
  346.3 0.6 maximum_bitcast_fusion.1
  (29 shorter events, 0.9 us)
Async XLA Ops:
  7.2 2.6 copy-start.2
  7.2 2.6 copy-start.6
  7.2 60.2 %all-gather.6.cloned.1.call-start = ((), (), s32[]{:S(2)}) async-start(), calls=%async_computation | async-start | bytes 2359296 | tf_op jit(solution)/shard_map/all_gather | solution.py:53
  9.8 18.5 %copy-start.3 = (bf16[1,5,128,1024]{3,2,1,0:T(8,128)(2,1)S(1)}, bf16[1,5,128,1024]{3,2,1,0:T(8,128)(2,1)}, u32[]{:S(2)}) copy-start(bf16[1,5,128,1024]{3,2,1,0:T(8,128)(2,1)} %param.7) | copy-start | bytes 3932164
  28.2 75.2 %all-gather.8.cloned.1.call-start = ((), (), s32[]{:S(2)}) async-start(), calls=%async_computation.1 | async-start | bytes 7077888 | tf_op jit(solution)/shard_map/all_gather | solution.py:26
  28.4 20.8 %copy-start.4 = (bf16[1,5,128,1024]{3,2,1,0:T(8,128)(2,1)S(1)}, bf16[1,5,128,1024]{3,2,1,0:T(8,128)(2,1)}, u32[]{:S(2)}) copy-start(bf16[1,5,128,1024]{3,2,1,0:T(8,128)(2,1)} %param.6) | copy-start | bytes 3932164
  28.5 19.7 %collective-permute-start.1 = (bf16[3,128,1024]{2,1,0:T(8,128)(2,1)S(1)}, bf16[3,128,1024]{2,1,0:T(8,128)(2,1)S(1)}, u32[]{:S(2)}, u32[]{:S(2)}) collective-permute-start(bf16[3,128,1024]{2,1,0:T(8,128)(2,1)S(1)} %pad_maximum_fusion.1), channel_id=1, source_target_pairs={{0,24},{8,0},{16,8},{24,16},{1,25},{9,1},{17,9},{25,17},{2,26},{10... | collective-permute-start | bytes 2359304 | tf_op jit(solution)/shard_map/ppermute | solution.py:16
  48.2 0.9 copy-start.5
  49.1 121.7 %all-gather.10.cloned.1.call-start = ((), (), s32[]{:S(2)}) async-start(), calls=%async_computation.2 | async-start | bytes 2359296 | tf_op jit(solution)/shard_map/all_gather | solution.py:53
  49.3 18.1 %collective-permute-start = (bf16[3,128,1024]{2,1,0:T(8,128)(2,1)S(1)}, bf16[3,128,1024]{2,1,0:T(8,128)(2,1)S(1)}, u32[]{:S(2)}, u32[]{:S(2)}) collective-permute-start(bf16[3,128,1024]{2,1,0:T(8,128)(2,1)S(1)} %pad_maximum_fusion), channel_id=1, source_target_pairs={{0,8},{8,16},{16,24},{24,0},{1,9},{9,17},{17,25},{25,1},{2,10},{10... | collective-permute-start | bytes 2359304 | tf_op jit(solution)/shard_map/ppermute | solution.py:16
  103.4 4.7 %copy-start.1 = (bf16[3,1024,1024]{2,1,0:T(8,128)(2,1)S(1)}, bf16[3,1024,1024]{2,1,0:T(8,128)(2,1)}, u32[]{:S(2)}) copy-start(bf16[3,1024,1024]{2,1,0:T(8,128)(2,1)} %all-gather.8.cloned.1.call-done) | copy-start | bytes 18874372
  109.2 4.0 %copy-start = (bf16[5120,1024]{1,0:T(8,128)(2,1)}, bf16[5120,1024]{1,0:T(8,128)(2,1)S(1)}, u32[]{:S(2)}) copy-start(bf16[5120,1024]{1,0:T(8,128)(2,1)S(1)} %fusion.6) | copy-start | bytes 31457284
  142.9 95.3 %all-gather.12.cloned.1.call-start = ((), (), s32[]{:S(2)}) async-start(), calls=%async_computation.3 | async-start | bytes 2359296 | tf_op jit(solution)/shard_map/all_gather | solution.py:53
  210.3 95.3 %all-gather.14.cloned.1.call-start = ((), (), s32[]{:S(2)}) async-start(), calls=%async_computation.4 | async-start | bytes 2359296 | tf_op jit(solution)/shard_map/all_gather | solution.py:53
Sparse Core Ops, SparseCore 0:
  28.3 27.1 all-gather.5
  58.0 45.3 all-gather.7
  143.0 27.7 all-gather.9
  210.4 27.7 all-gather.11
  277.8 27.7 all-gather.13

commit v2 on v1

v2 whole, which is shorter than its diff:
```python
import functools

import jax
import jax.numpy as jnp
from jax import lax
from jax.experimental import pallas as pl
from jax.experimental.pallas import tpu as pltpu
from jax.sharding import PartitionSpec as P

CHI = 1024
ITERS = 4
EPS = 1e-06
MESH = pl.DeviceIdType.MESH
TILE = 256


def merged(env):
    return jnp.stack([env[0] + env[1] + env[2], env[3], env[4]])


def kernel(
    n,
    segs,
    left_ref,
    right_ref,
    start_ref,
    row_ref,
    col_ref,
    mine_ref,
    final_ref,
    beta_ref,
    left_buf,
    raw,
    split,
    whole,
    first,
    mixed,
    current,
    previous,
    vector,
    parts,
    left_send,
    left_recv,
    shift_send,
    shift_recv,
    right_send,
    right_recv,
    pass_send,
    pass_recv,
    vec_send,
    vec_recv,
    fwd_send,
    fwd_recv,
    part_send,
    part_recv,
):
    me = lax.axis_index("sec")
    seg = lax.axis_index("seg")
    rows, width = start_ref.shape
    chips = n // 2
    partner = me + 1 - 2 * lax.rem(me, 2)
    after, before = lax.rem(seg + 1, segs), lax.rem(seg + segs - 1, segs)

    def source(k):
        return lax.rem(me - 2 * k + n, n)

    def target(k):
        return lax.rem(me + 2 * k, n)

    def block(index):
        return pl.ds(pl.multiple_of(index * rows, rows), rows)

    barrier = pltpu.get_barrier_semaphore()
    for k in range(1, n):
        pl.semaphore_signal(barrier, inc=1, device_id={"sec": lax.rem(me + k, n)}, device_id_type=MESH)
    for other in (after, before):
        pl.semaphore_signal(barrier, inc=1, device_id={"seg": other}, device_id_type=MESH)
    pl.semaphore_wait(barrier, n + 1)

    def remote(src, dst, send, recv, where):
        return pltpu.make_async_remote_copy(
            src_ref=src, dst_ref=dst, send_sem=send, recv_sem=recv, device_id=where, device_id_type=MESH
        )

    left_copy = remote(left_ref, left_buf, left_send, left_recv, {"seg": after})
    shifts = [
        remote(right_ref.at[c], raw.at[c, block(me)], shift_send.at[c], shift_recv.at[c], {"seg": before})
        for c in range(3)
    ]

    def right_copy(c, k, owner):
        part = raw.at[c, block(owner)]
        return remote(part, part, right_send.at[c, k], right_recv.at[c, k], {"sec": target(k)})

    def right_pass(c, k):
        part = raw.at[c, block(source(k))]
        return remote(part, part, pass_send.at[c, k], pass_recv.at[c, k], {"sec": partner})

    def vec_copy(it, k):
        part = whole.at[it, block(me)]
        return remote(part, part, vec_send.at[it, k], vec_recv.at[it, k], {"sec": target(k)})

    def vec_pass(it, k):
        part = whole.at[it, block(source(k))]
        return remote(part, part, fwd_send.at[it, k], fwd_recv.at[it, k], {"sec": partner})

    def part_copy(slot, k):
        part = parts.at[slot, me]
        return remote(part, part, part_send.at[slot, k], part_recv.at[slot, k], {"sec": lax.rem(me + k, n)})

    def fold(value):
        total = value[0:8]
        for r in range(8, rows, 8):
            total = total + value[r : r + 8]
        short = total[:, 0:128]
        for c in range(128, value.shape[1], 128):
            short = short + total[:, c : c + 128]
        return short

    def send_part(slot, tile):
        parts[slot, me] = tile
        for k in range(1, n):
            part_copy(slot, k).start()

    def total_of(slot):
        for k in range(1, n):
            part_copy(slot, k).wait()
        total = parts[slot, 0]
        for j in range(1, n):
            total = total + parts[slot, j]
        return jnp.sum(total)

    def send_vector(it):
        for t in range(0, width, TILE):
            whole[it, block(me), t : t + TILE] = vector[:, t : t + TILE].astype(jnp.bfloat16)
        for k in range(1, chips):
            vec_copy(it, k).start()
        vec_pass(it, 0).start()

    for copy in shifts:
        copy.start()

    tile = jnp.zeros((8, 128), jnp.float32)
    for t in range(0, width, TILE):
        piece = start_ref[:, t : t + TILE]
        vector[:, t : t + TILE] = piece
        previous[:, t : t + TILE] = jnp.zeros_like(piece)
        tile = tile + fold(piece * piece)
    send_part(0, tile)
    send_vector(0)

    for c in range(3):
        shifts[c].wait()
        for k in range(1, chips):
            right_copy(c, k, me).start()
        right_pass(c, 0).start()
        if c == 2:
            left_copy.start()
        if c > 0:
            for k in range(1, chips):
                right_copy(c - 1, k, me).wait()
                right_pass(c - 1, k).start()
    for k in range(1, chips):
        right_copy(2, k, me).wait()
        right_pass(2, k).start()
    for c in range(3):
        for k in range(chips):
            right_pass(c, k).wait()

    charges = row_ref[...]

    @pl.loop(0, width // 128)
    def _(b):
        lines = pl.ds(pl.multiple_of(b * 128, 128), 128)
        step = charges - col_ref[lines, :]
        value = raw[0, lines, :].astype(jnp.float32)
        split[0, lines, :] = jnp.where(step == 0, value, 0.0).astype(jnp.bfloat16)
        split[1, lines, :] = jnp.where(step == 1, value, 0.0).astype(jnp.bfloat16)
        split[2, lines, :] = jnp.where(step == -1, value, 0.0).astype(jnp.bfloat16)

    left_copy.wait()

    def iteration(it, carry):
        def at(t):
            return pl.ds(pl.multiple_of(t * TILE, TILE), TILE)

        for k in range(chips):
            if k > 0:
                vec_copy(it, k).wait()
                vec_pass(it, k).start()
            vec_pass(it, k).wait()
            chip = lax.rem(me // 2 - k + chips, chips)
            span = pl.ds(pl.multiple_of(chip * 2 * rows, 2 * rows), 2 * rows)

            @pl.loop(0, width // TILE)
            def _(t, k=k, span=span):
                product = jnp.dot(
                    left_buf[:, span], whole[it, span, at(t)], preferred_element_type=jnp.float32
                )
                if k > 0:
                    product = product + first[:, at(t)]
                first[:, at(t)] = product

        size = jnp.sqrt(jnp.full((1, 128), total_of(2 * it) + EPS, jnp.float32))
        beta_ref[pl.ds(it, 1), :] = size
        size = size[:, 0:1]
        inverse = 1.0 / size

        @pl.loop(0, width // TILE)
        def _(t):
            gap = row_ref[:, at(t)] - mine_ref[...]
            up, down = gap == 1, gap == 0
            allowed = jnp.logical_or(up, down)
            spin = jnp.where(up, 0.5, -0.5)
            a = first[0:rows, at(t)] * inverse
            b = first[rows : 2 * rows, at(t)] * inverse
            c = first[2 * rows : 3 * rows, at(t)] * inverse
            half = 0.5 * c
            mixed[0, :, at(t)] = jnp.where(allowed, a + spin * b, 0.0).astype(jnp.bfloat16)
            mixed[1, :, at(t)] = jnp.where(up, half, 0.0).astype(jnp.bfloat16)
            mixed[2, :, at(t)] = jnp.where(down, half, 0.0).astype(jnp.bfloat16)
            mixed[3, :, at(t)] = jnp.where(allowed, spin * c, 0.0).astype(jnp.bfloat16)
            mixed[4, :, at(t)] = jnp.where(allowed, c, 0.0).astype(jnp.bfloat16)
            current[:, at(t)] = vector[:, at(t)] * inverse

        def second(t, tile):
            image = jnp.dot(mixed[0], split[0, :, at(t)], preferred_element_type=jnp.float32)
            image = image + jnp.dot(mixed[1], split[1, :, at(t)], preferred_element_type=jnp.float32)
            image = image + jnp.dot(mixed[2], split[2, :, at(t)], preferred_element_type=jnp.float32)
            image = image + jnp.dot(mixed[3], raw[1, :, at(t)], preferred_element_type=jnp.float32)
            image = image + jnp.dot(mixed[4], raw[2, :, at(t)], preferred_element_type=jnp.float32)
            gap = row_ref[:, at(t)] - mine_ref[...]
            allowed = jnp.logical_or(gap == 1, gap == 0)
            residual = jnp.where(allowed, image, 0.0) - size * previous[:, at(t)]
            vector[:, at(t)] = residual
            return tile + fold(residual * current[:, at(t)])

        tile = lax.fori_loop(0, width // TILE, second, jnp.zeros((8, 128), jnp.float32))
        send_part(2 * it + 1, tile)
        alpha = jnp.full((1, 1), total_of(2 * it + 1), jnp.float32)

        def finish(t, tile):
            now = current[:, at(t)]
            residual = vector[:, at(t)] - alpha * now
            vector[:, at(t)] = residual
            previous[:, at(t)] = now
            return tile + fold(residual * residual)

        tile = lax.fori_loop(0, width // TILE, finish, jnp.zeros((8, 128), jnp.float32))
        send_part(2 * it + 2, tile)

        @pl.when(it < ITERS - 1)
        def _():
            send_vector(it + 1)

        return carry

    lax.fori_loop(0, ITERS, iteration, 0)

    size = jnp.sqrt(jnp.full((1, 128), total_of(2 * ITERS) + EPS, jnp.float32))
    beta_ref[ITERS : ITERS + 1, :] = size
    scale = CHI / size[:, 0:1]
    for t in range(0, width, TILE):
        final_ref[:, t : t + TILE] = vector[:, t : t + TILE] * scale


def on_device(n, segs, start_vector, left_env, right_env, charge_left, charge_right):
    rows, width = left_env.shape[2], left_env.shape[3]
    left = merged(left_env[0]).reshape(3 * rows, width)
    right = merged(right_env[0])
    line = charge_right[0][None, :]
    mine = charge_left[0][:, None]
    gap = line - mine
    down, up = gap == 0, gap == 1
    start = jnp.where(down, start_vector[0, :, 0], jnp.where(up, start_vector[0, :, 1], 0.0))
    slots = 2 * ITERS + 1
    chips = n // 2
    dma = pltpu.SemaphoreType.DMA
    final, betas = pl.pallas_call(
        functools.partial(kernel, n, segs),
        out_shape=(
            jax.ShapeDtypeStruct((rows, width), jnp.float32),
            jax.ShapeDtypeStruct((8, 128), jnp.float32),
        ),
        in_specs=[pl.BlockSpec(memory_space=pltpu.VMEM)] * 6,
        out_specs=[pl.BlockSpec(memory_space=pltpu.VMEM)] * 2,
        scratch_shapes=[
            pltpu.VMEM((3 * rows, width), jnp.bfloat16),
            pltpu.VMEM((3, n * rows, width), jnp.bfloat16),
            pltpu.VMEM((3, n * rows, width), jnp.bfloat16),
            pltpu.VMEM((ITERS, n * rows, width), jnp.bfloat16),
            pltpu.VMEM((3 * rows, width), jnp.float32),
            pltpu.VMEM((5, rows, width), jnp.bfloat16),
            pltpu.VMEM((rows, width), jnp.float32),
            pltpu.VMEM((rows, width), jnp.float32),
            pltpu.VMEM((rows, width), jnp.float32),
            pltpu.VMEM((slots, n, 8, 128), jnp.float32),
            dma,
            dma,
            dma((3,)),
            dma((3,)),
            dma((3, chips)),
            dma((3, chips)),
            dma((3, chips)),
            dma((3, chips)),
            dma((ITERS, chips)),
            dma((ITERS, chips)),
            dma((ITERS, chips)),
            dma((ITERS, chips)),
            dma((slots, n)),
            dma((slots, n)),
        ],
        compiler_params=pltpu.CompilerParams(
            collective_id=0, has_side_effects=True, vmem_limit_bytes=48 * 1024 * 1024
        ),
    )(left, right, start, line, line.reshape(width, 1), mine)
    full = jnp.stack([jnp.where(down, final, 0.0), jnp.where(up, final, 0.0)], axis=1)
    return full[None], betas[None, 1 : ITERS + 1, 0]


def solution(mesh):
    return jax.shard_map(
        functools.partial(on_device, mesh.shape["sec"], mesh.shape["seg"]),
        mesh=mesh,
        in_specs=(
            P("seg", "sec", None, None),
            P("seg", None, "sec", None),
            P("seg", None, "sec", None),
            P("seg", "sec"),
            P("seg", None),
        ),
        out_specs=(P("seg", "sec", None, None), P("seg", None)),
        check_vma=False,
    )
```

time: 354 us -> 156 us (0.44)
  waiting for transfers between devices: 150 us -> 0 us
  Pallas kernels: 0 us -> 147 us
  blocking collectives: 120 us -> 0 us
  matrix products: 32.1 us -> 0 us
  other arithmetic: 22.3 us -> 2.08 us
  between operations: 17.6 us -> 0.74 us
  starting transfers between devices: 4.1 us -> 0 us
    pallas_call x0 -> x1, Pallas kernels: none -> 147 us  [on_device(): pl.pallas_call(functools.partial(kernel, n, segs), out_shape=(jax.ShapeDt...]
    psum x9 -> x0, blocking collectives: 120 us -> none  [the longest x4 54.8 us: on_device(): alpha = lax.psum(jnp.sum(residual * current), 'sec')]
    all_gather x5 -> x0, waiting for transfers between devices: 116 us -> none  [the longest x4 83.5 us: on_device(): lax.all_gather(current.astype(jnp.bfloat16), 'sec', axis=0, tiled=True)]
    ppermute x2 -> x0, waiting for transfers between devices: 34.1 us -> none  [shifted(): return lax.ppermute(value, axis, pairs)]
    dot_general x8 -> x0, matrix products: 32.1 us -> none  [the longest x4 21.8 us: on_device(): image = jnp.dot(mixed, right_stack, preferred_element_type=jnp.float32)]
    unnamed x19 -> x0, other arithmetic: 8.02 us -> none
    reduce_sum x5 -> x0, other arithmetic: 6.53 us -> none  [the longest x4 5.56 us: on_device(): beta = jnp.sqrt(lax.psum(jnp.sum(residual * residual), 'sec') + EPS)]
    convert_element_type x4 -> x0, other arithmetic: 5.36 us -> none  [on_device(): current.astype(jnp.bfloat16)]
  transfers between devices with their start and end apart: 7 -> 0, of which waited for: 6 -> 0; matrix products, arithmetic and copies ran while one was open for 1% -> 0% of each run, Pallas kernels for 0% -> 0%
where the time goes in v2:
time: 156 us
  Pallas kernels  147 us (94%)
  local copies, waits for them, and re-layouts  5.87 us (4%)
  other arithmetic  2.08 us (1%)
    pallas_call x1, Pallas kernels, on_device(): pl.pallas_call(functools.partial(kernel, n, segs), out_shape=(jax.ShapeDt...  147 us
    unnamed x9, local copies, waits for them, and re-layouts  4.11 us

profile of v2, /device:TPU:0, one launch (start us, length us, event | category | flops | bytes accessed | tf_op | source)
XLA Modules:
  0.0 156.2 jit_solution(18296580308187960667)
XLA Ops:
  0.6 1.3 add_bitcast_fusion
  2.0 0.0 copy-start.1
  2.0 0.1 pad_maximum_fusion.1.right_ref
  2.1 1.2 copy-done.1
  3.3 0.1 add_bitcast_fusion.1
  3.4 0.0 copy-start.2
  3.4 0.1 pad_maximum_fusion
  3.5 0.0 copy-start
  3.5 0.0 copy-start.3
  3.5 1.1 copy-done.2
  4.6 0.8 fusion.6
  5.4 0.0 copy-done
  5.4 0.0 copy-done.3
  5.4 0.3 fusion.1.start_ref
  5.7 0.2 copy.13.col_ref
  5.9 0.1 copy.14.mine_ref
  6.0 147.5 %shard_map.68 = (f32[128,1024]{1,0:T(8,128)S(1)}, f32[8,128]{1,0:T(8,128)S(1)}) custom-call(bf16[384,1024]{1,0:T(8,128)(2,1)S(1)} %bitcast.32, bf16[3,128,1024]{2,1,0:T(8,128)(2,1)S(1)} %pad_maximum_fusion.1.right_ref, f32[128,1024]{1,0:T(8,128)S(1)} %fusion.1.start_ref, s32[1,1024]{1,0:T(1,128)S(1)} %copy-done, s32[1024,1]{1,0:T(8,128)S(1)} %copy.13.col_ref, ...), custom_call_target="tpu_custom_call" | custom-call | tf_op jit(solution)/shard_map/pallas_call | solution.py:279
  153.5 0.2 fusion.5
  153.7 0.1 maximum_bitcast_fusion
  153.7 1.8 %copy.15 = f32[1,128,2,1024]{3,2,1,0:T(2,128)} copy(f32[1,128,2,1024]{3,1,2,0:T(8,128)S(1)} %maximum_bitcast_fusion) | data formatting | bytes 2097152
  155.5 0.6 slice_reduce_fusion
Async XLA Ops:
  2.0 1.3 copy-start.1
  3.4 1.2 copy-start.2
  3.5 1.9 %copy-start = (s32[1,1024]{1,0:T(1,128)S(1)}, s32[1,1024]{1,0:T(1,128)}, u32[]{:S(2)}) copy-start(s32[1,1024]{1,0:T(1,128)} %row_ref.1) | copy-start | bytes 12292
  3.5 1.9 %copy-start.3 = (s32[1,128]{1,0:T(1,128)S(1)}, s32[1,128]{1,0:T(1,128)}, u32[]{:S(2)}) copy-start(s32[1,128]{1,0:T(1,128)} %param.8) | copy-start | bytes 1540

commit v3 on v2

--- a/solution.py
+++ b/solution.py
@@ -61,6 +61,15 @@
     partner = me + 1 - 2 * lax.rem(me, 2)
     after, before = lax.rem(seg + 1, segs), lax.rem(seg + segs - 1, segs)
 
+    square = chips == 4
+    pieces = 7 if square else chips
+    if square:
+        column = lax.rem(me // 2, 2)
+        line = me // 4
+        beside = me + 2 - 4 * column
+        above = me + 4 - 8 * line
+        across = above + 2 - 4 * column
+
     def source(k):
         return lax.rem(me - 2 * k + n, n)
 
@@ -88,21 +97,57 @@
         for c in range(3)
     ]
 
-    def right_copy(c, k, owner):
-        part = raw.at[c, block(owner)]
-        return remote(part, part, right_send.at[c, k], right_recv.at[c, k], {"sec": target(k)})
-
-    def right_pass(c, k):
-        part = raw.at[c, block(source(k))]
-        return remote(part, part, pass_send.at[c, k], pass_recv.at[c, k], {"sec": partner})
-
-    def vec_copy(it, k):
-        part = whole.at[it, block(me)]
-        return remote(part, part, vec_send.at[it, k], vec_recv.at[it, k], {"sec": target(k)})
-
-    def vec_pass(it, k):
-        part = whole.at[it, block(source(k))]
-        return remote(part, part, fwd_send.at[it, k], fwd_recv.at[it, k], {"sec": partner})
+    class Gather:
+        def __init__(self, buf, i, send, recv, fsend, frecv):
+            self.buf, self.i = buf, i
+            self.sems = send, recv, fsend, frecv
+
+        def move(self, j, owner, half, where, forward=False):
+            send, recv = self.sems[2:] if forward else self.sems[:2]
+            if half is None:
+                part = self.buf.at[self.i, block(owner)]
+            else:
+                size = rows // 2
+                part = self.buf.at[self.i, pl.ds(pl.multiple_of(owner * rows + half * size, size), size)]
+            return remote(part, part, send.at[self.i, j], recv.at[self.i, j], {"sec": where})
+
+        def direct(self, j):
+            if not square:
+                return self.move(j, me, None, target(j))
+            return self.move(j, me, (0, 1, 1, 0)[j - 1], (beside, above)[(j - 1) % 2])
+
+        def relay(self, j):
+            return self.move(5 + j, (beside, above)[j], j, (above, beside)[j])
+
+        def passed(self, j):
+            if not square:
+                return self.move(j, source(j), None, partner, True)
+            owner = (me, beside, above, beside, above, across, across)[j]
+            return self.move(j, owner, (None, 0, 1, 1, 0, 0, 1)[j], partner, True)
+
+        def begin(self):
+            for j in range(1, 5 if square else chips):
+                self.direct(j).start()
+            self.passed(0).start()
+
+        def spread(self):
+            for j in range(1, 5 if square else chips):
+                self.direct(j).wait()
+                if square and j < 3:
+                    self.relay(j - 1).start()
+                self.passed(j).start()
+
+        def last(self):
+            if square:
+                for j in range(2):
+                    self.relay(j).wait()
+                    self.passed(5 + j).start()
+
+    def right_gather(c):
+        return Gather(raw, c, right_send, right_recv, pass_send, pass_recv)
+
+    def vector_gather(it):
+        return Gather(whole, it, vec_send, vec_recv, fwd_send, fwd_recv)
 
     def part_copy(slot, k):
         part = parts.at[slot, me]
@@ -117,25 +162,27 @@
             short = short + total[:, c : c + 128]
         return short
 
-    def send_part(slot, tile):
-        parts[slot, me] = tile
+    def send_part(slot, tile, other=None):
+        parts[slot, me, 0:8] = tile
+        parts[slot, me, 8:16] = jnp.zeros_like(tile) if other is None else other
         for k in range(1, n):
             part_copy(slot, k).start()
 
-    def total_of(slot):
+    def totals_of(slot):
         for k in range(1, n):
             part_copy(slot, k).wait()
         total = parts[slot, 0]
         for j in range(1, n):
             total = total + parts[slot, j]
-        return jnp.sum(total)
-
-    def send_vector(it):
+        return jnp.sum(total[0:8]), jnp.sum(total[8:16])
+
+    def send_vector(it, factor):
         for t in range(0, width, TILE):
-            whole[it, block(me), t : t + TILE] = vector[:, t : t + TILE].astype(jnp.bfloat16)
-        for k in range(1, chips):
-            vec_copy(it, k).start()
-        vec_pass(it, 0).start()
+            whole[it, block(me), t : t + TILE] = (vector[:, t : t + TILE] * factor).astype(jnp.bfloat16)
+        vector_gather(it).begin()
+
+    def root(value):
+        return jnp.sqrt(jnp.full((1, 128), value + EPS, jnp.float32))
 
     for copy in shifts:
         copy.start()
@@ -146,26 +193,26 @@
         vector[:, t : t + TILE] = piece
         previous[:, t : t + TILE] = jnp.zeros_like(piece)
         tile = tile + fold(piece * piece)
+    send_part(2 * ITERS + 1, tile)
+    guess = root(totals_of(2 * ITERS + 1)[0])
     send_part(0, tile)
-    send_vector(0)
+    send_vector(0, 1.0 / guess[:, 0:1])
 
     for c in range(3):
         shifts[c].wait()
-        for k in range(1, chips):
-            right_copy(c, k, me).start()
-        right_pass(c, 0).start()
+        right_gather(c).begin()
         if c == 2:
             left_copy.start()
         if c > 0:
-            for k in range(1, chips):
-                right_copy(c - 1, k, me).wait()
-                right_pass(c - 1, k).start()
-    for k in range(1, chips):
-        right_copy(2, k, me).wait()
-        right_pass(2, k).start()
+            right_gather(c - 1).spread()
+        if c > 1:
+            right_gather(c - 2).last()
+    right_gather(2).spread()
+    right_gather(1).last()
+    right_gather(2).last()
     for c in range(3):
-        for k in range(chips):
-            right_pass(c, k).wait()
+        for j in range(pieces):
+            right_gather(c).passed(j).wait()
 
     charges = row_ref[...]
 
@@ -180,31 +227,45 @@
 
     left_copy.wait()
 
-    def iteration(it, carry):
+    def iteration(it, guess):
         def at(t):
             return pl.ds(pl.multiple_of(t * TILE, TILE), TILE)
 
-        for k in range(chips):
-            if k > 0:
-                vec_copy(it, k).wait()
-                vec_pass(it, k).start()
-            vec_pass(it, k).wait()
-            chip = lax.rem(me // 2 - k + chips, chips)
-            span = pl.ds(pl.multiple_of(chip * 2 * rows, 2 * rows), 2 * rows)
+        def contract(owner, fresh):
+            span = pl.ds(pl.multiple_of(owner // 2 * (2 * rows), 2 * rows), 2 * rows)
 
             @pl.loop(0, width // TILE)
-            def _(t, k=k, span=span):
+            def _(t):
                 product = jnp.dot(
                     left_buf[:, span], whole[it, span, at(t)], preferred_element_type=jnp.float32
                 )
-                if k > 0:
+                if not fresh:
                     product = product + first[:, at(t)]
                 first[:, at(t)] = product
 
-        size = jnp.sqrt(jnp.full((1, 128), total_of(2 * it) + EPS, jnp.float32))
+        gather = vector_gather(it)
+        gather.passed(0).wait()
+        contract(me, True)
+        gather.spread()
+        if square:
+            for owner, own in ((beside, (1, 3)), (above, (2, 4))):
+                for j in own:
+                    gather.passed(j).wait()
+                contract(owner, False)
+            gather.last()
+            for j in (5, 6):
+                gather.passed(j).wait()
+            contract(across, False)
+        else:
+            for k in range(1, chips):
+                gather.passed(k).wait()
+                contract(source(k), False)
+
+        size = root(totals_of(2 * it)[0])
         beta_ref[pl.ds(it, 1), :] = size
         size = size[:, 0:1]
         inverse = 1.0 / size
+        ratio = guess[:, 0:1] * inverse
 
         @pl.loop(0, width // TILE)
         def _(t):
@@ -212,9 +273,9 @@
             up, down = gap == 1, gap == 0
             allowed = jnp.logical_or(up, down)
             spin = jnp.where(up, 0.5, -0.5)
-            a = first[0:rows, at(t)] * inverse
-            b = first[rows : 2 * rows, at(t)] * inverse
-            c = first[2 * rows : 3 * rows, at(t)] * inverse
+            a = first[0:rows, at(t)] * ratio
+            b = first[rows : 2 * rows, at(t)] * ratio
+            c = first[2 * rows : 3 * rows, at(t)] * ratio
             half = 0.5 * c
             mixed[0, :, at(t)] = jnp.where(allowed, a + spin * b, 0.0).astype(jnp.bfloat16)
             mixed[1, :, at(t)] = jnp.where(up, half, 0.0).astype(jnp.bfloat16)
@@ -223,7 +284,7 @@
             mixed[4, :, at(t)] = jnp.where(allowed, c, 0.0).astype(jnp.bfloat16)
             current[:, at(t)] = vector[:, at(t)] * inverse
 
-        def second(t, tile):
+        def second(t, tiles):
             image = jnp.dot(mixed[0], split[0, :, at(t)], preferred_element_type=jnp.float32)
             image = image + jnp.dot(mixed[1], split[1, :, at(t)], preferred_element_type=jnp.float32)
             image = image + jnp.dot(mixed[2], split[2, :, at(t)], preferred_element_type=jnp.float32)
@@ -233,11 +294,13 @@
             allowed = jnp.logical_or(gap == 1, gap == 0)
             residual = jnp.where(allowed, image, 0.0) - size * previous[:, at(t)]
             vector[:, at(t)] = residual
-            return tile + fold(residual * current[:, at(t)])
-
-        tile = lax.fori_loop(0, width // TILE, second, jnp.zeros((8, 128), jnp.float32))
-        send_part(2 * it + 1, tile)
-        alpha = jnp.full((1, 1), total_of(2 * it + 1), jnp.float32)
+            return tiles[0] + fold(residual * current[:, at(t)]), tiles[1] + fold(residual * residual)
+
+        zero = jnp.zeros((8, 128), jnp.float32)
+        send_part(2 * it + 1, *lax.fori_loop(0, width // TILE, second, (zero, zero)))
+        product, square_sum = totals_of(2 * it + 1)
+        alpha = jnp.full((1, 1), product, jnp.float32)
+        guess = root(jnp.maximum(square_sum - product * product, 0.0))
 
         def finish(t, tile):
             now = current[:, at(t)]
@@ -246,18 +309,18 @@
             previous[:, at(t)] = now
             return tile + fold(residual * residual)
 
-        tile = lax.fori_loop(0, width // TILE, finish, jnp.zeros((8, 128), jnp.float32))
-        send_part(2 * it + 2, tile)
+        tile = lax.fori_loop(0, width // TILE, finish, zero)
 
         @pl.when(it < ITERS - 1)
         def _():
-            send_vector(it + 1)
-
-        return carry
-
-    lax.fori_loop(0, ITERS, iteration, 0)
-
-    size = jnp.sqrt(jnp.full((1, 128), total_of(2 * ITERS) + EPS, jnp.float32))
+            send_vector(it + 1, 1.0 / guess[:, 0:1])
+
+        send_part(2 * it + 2, tile)
+        return guess
+
+    lax.fori_loop(0, ITERS, iteration, guess)
+
+    size = root(totals_of(2 * ITERS)[0])
     beta_ref[ITERS : ITERS + 1, :] = size
     scale = CHI / size[:, 0:1]
     for t in range(0, width, TILE):
@@ -273,8 +336,8 @@
     gap = line - mine
     down, up = gap == 0, gap == 1
     start = jnp.where(down, start_vector[0, :, 0], jnp.where(up, start_vector[0, :, 1], 0.0))
-    slots = 2 * ITERS + 1
-    chips = n // 2
+    slots = 2 * ITERS + 2
+    pieces = 7 if n == 8 else n // 2
     dma = pltpu.SemaphoreType.DMA
     final, betas = pl.pallas_call(
         functools.partial(kernel, n, segs),
@@ -294,19 +357,19 @@
             pltpu.VMEM((rows, width), jnp.float32),
             pltpu.VMEM((rows, width), jnp.float32),
             pltpu.VMEM((rows, width), jnp.float32),
-            pltpu.VMEM((slots, n, 8, 128), jnp.float32),
+            pltpu.VMEM((slots, n, 16, 128), jnp.float32),
             dma,
             dma,
             dma((3,)),
             dma((3,)),
-            dma((3, chips)),
-            dma((3, chips)),
-            dma((3, chips)),
-            dma((3, chips)),
-            dma((ITERS, chips)),
-            dma((ITERS, chips)),
-            dma((ITERS, chips)),
-            dma((ITERS, chips)),
+            dma((3, pieces)),
+            dma((3, pieces)),
+            dma((3, pieces)),
+            dma((3, pieces)),
+            dma((ITERS, pieces)),
+            dma((ITERS, pieces)),
+            dma((ITERS, pieces)),
+            dma((ITERS, pieces)),
             dma((slots, n)),
             dma((slots, n)),
         ],

time: 156 us -> 135 us (0.87)
  Pallas kernels: 147 us -> 126 us
    pallas_call x1, Pallas kernels: 147 us -> 126 us  [on_device(): pl.pallas_call(functools.partial(kernel, n, segs), out_shape=(jax.ShapeDt...]
where the time goes in v3:
time: 135 us
  Pallas kernels  126 us (93%)
  local copies, waits for them, and re-layouts  5.87 us (4%)
  other arithmetic  2.08 us (2%)
    pallas_call x1, Pallas kernels, on_device(): pl.pallas_call(functools.partial(kernel, n, segs), out_shape=(jax.ShapeDt...  126 us
    unnamed x9, local copies, waits for them, and re-layouts  4.11 us

profile of v3, /device:TPU:0, one launch (start us, length us, event | category | flops | bytes accessed | tf_op | source)
XLA Modules:
  0.0 135.1 jit_solution(7499155094101989526)
XLA Ops:
  0.6 1.3 add_bitcast_fusion
  2.0 0.0 copy-start.1
  2.0 0.1 pad_maximum_fusion.1.right_ref
  2.1 1.2 copy-done.1
  3.3 0.1 add_bitcast_fusion.1
  3.4 0.0 copy-start.2
  3.4 0.1 pad_maximum_fusion
  3.5 0.0 copy-start
  3.5 0.0 copy-start.3
  3.5 1.1 copy-done.2
  4.6 0.8 fusion.6
  5.4 0.0 copy-done
  5.4 0.0 copy-done.3
  5.4 0.3 fusion.1.start_ref
  5.7 0.2 copy.13.col_ref
  5.9 0.1 copy.14.mine_ref
  6.0 126.4 %shard_map.68 = (f32[128,1024]{1,0:T(8,128)S(1)}, f32[8,128]{1,0:T(8,128)S(1)}) custom-call(bf16[384,1024]{1,0:T(8,128)(2,1)S(1)} %bitcast.32, bf16[3,128,1024]{2,1,0:T(8,128)(2,1)S(1)} %pad_maximum_fusion.1.right_ref, f32[128,1024]{1,0:T(8,128)S(1)} %fusion.1.start_ref, s32[1,1024]{1,0:T(1,128)S(1)} %copy-done, s32[1024,1]{1,0:T(8,128)S(1)} %copy.13.col_ref, ...), custom_call_target="tpu_custom_call" | custom-call | tf_op jit(solution)/shard_map/pallas_call | solution.py:342
  132.4 0.2 fusion.5
  132.6 0.1 maximum_bitcast_fusion
  132.7 1.8 %copy.15 = f32[1,128,2,1024]{3,2,1,0:T(2,128)} copy(f32[1,128,2,1024]{3,1,2,0:T(8,128)S(1)} %maximum_bitcast_fusion) | data formatting | bytes 2097152
  134.5 0.6 slice_reduce_fusion
Async XLA Ops:
  2.0 1.3 copy-start.1
  3.4 1.2 copy-start.2
  3.5 1.9 %copy-start = (s32[1,1024]{1,0:T(1,128)S(1)}, s32[1,1024]{1,0:T(1,128)}, u32[]{:S(2)}) copy-start(s32[1,1024]{1,0:T(1,128)} %row_ref.1) | copy-start | bytes 12292
  3.5 1.9 %copy-start.3 = (s32[1,128]{1,0:T(1,128)S(1)}, s32[1,128]{1,0:T(1,128)}, u32[]{:S(2)}) copy-start(s32[1,128]{1,0:T(1,128)} %param.8) | copy-start | bytes 1540

commit v4 on v3

--- a/solution.py
+++ b/solution.py
@@ -11,7 +11,7 @@
 ITERS = 4
 EPS = 1e-06
 MESH = pl.DeviceIdType.MESH
-TILE = 256
+TILE = 1024
 
 
 def merged(env):
@@ -201,7 +201,7 @@
     for c in range(3):
         shifts[c].wait()
         right_gather(c).begin()
-        if c == 2:
+        if c == 1:
             left_copy.start()
         if c > 0:
             right_gather(c - 1).spread()

time: 135 us -> 127 us (0.941)
  Pallas kernels: 126 us -> 118 us
    pallas_call x1, Pallas kernels: 126 us -> 118 us  [on_device(): pl.pallas_call(functools.partial(kernel, n, segs), out_shape=(jax.ShapeDt...]
where the time goes in v4:
time: 127 us
  Pallas kernels  118 us (93%)
  local copies, waits for them, and re-layouts  5.87 us (5%)
  other arithmetic  2.08 us (2%)
    pallas_call x1, Pallas kernels, on_device(): pl.pallas_call(functools.partial(kernel, n, segs), out_shape=(jax.ShapeDt...  118 us
    unnamed x9, local copies, waits for them, and re-layouts  4.11 us

profile of v4, /device:TPU:0, one launch (start us, length us, event | category | flops | bytes accessed | tf_op | source)
XLA Modules:
  0.0 127.1 jit_solution(2751817858700213519)
XLA Ops:
  0.6 1.3 %add_bitcast_fusion = (bf16[1,128,1024]{2,1,0:T(8,128)(2,1)S(1)}, bf16[1,128,1024]{2,1,0:T(8,128)(2,1)S(1)}, bf16[1,128,1024]{2,1,0:T(8,128)(2,1)S(1)}) fusion(bf16[1,5,128,1024]{3,2,1,0:T(8,128)(2,1)} %param.7), kind=kLoop, calls=%fused_computation.15 | loop fusion | flops 262144 | bytes 2097152 | tf_op jit(solution)/shard_map/add | solution.py:18
  2.0 0.0 copy-start.1
  2.0 0.1 pad_maximum_fusion.1.right_ref
  2.1 1.2 copy-done.1
  3.3 0.1 add_bitcast_fusion.1
  3.4 0.0 copy-start.2
  3.4 0.1 pad_maximum_fusion
  3.5 0.0 copy-start
  3.5 0.0 copy-start.3
  3.5 1.1 copy-done.2
  4.6 0.8 fusion.6
  5.4 0.0 copy-done
  5.4 0.0 copy-done.3
  5.4 0.3 fusion.1.start_ref
  5.7 0.2 copy.13.col_ref
  5.9 0.1 copy.14.mine_ref
  6.0 118.4 %shard_map.68 = (f32[128,1024]{1,0:T(8,128)S(1)}, f32[8,128]{1,0:T(8,128)S(1)}) custom-call(bf16[384,1024]{1,0:T(8,128)(2,1)S(1)} %bitcast.32, bf16[3,128,1024]{2,1,0:T(8,128)(2,1)S(1)} %pad_maximum_fusion.1.right_ref, f32[128,1024]{1,0:T(8,128)S(1)} %fusion.1.start_ref, s32[1,1024]{1,0:T(1,128)S(1)} %copy-done, s32[1024,1]{1,0:T(8,128)S(1)} %copy.13.col_ref, ...), custom_call_target="tpu_custom_call" | custom-call | tf_op jit(solution)/shard_map/pallas_call | solution.py:342
  124.4 0.2 fusion.5
  124.6 0.1 maximum_bitcast_fusion
  124.7 1.8 %copy.15 = f32[1,128,2,1024]{3,2,1,0:T(2,128)} copy(f32[1,128,2,1024]{3,1,2,0:T(8,128)S(1)} %maximum_bitcast_fusion) | data formatting | bytes 2097152
  126.5 0.6 slice_reduce_fusion
Async XLA Ops:
  2.0 1.3 %copy-start.1 = (bf16[1,5,128,1024]{3,2,1,0:T(8,128)(2,1)S(1)}, bf16[1,5,128,1024]{3,2,1,0:T(8,128)(2,1)}, u32[]{:S(2)}) copy-start(bf16[1,5,128,1024]{3,2,1,0:T(8,128)(2,1)} %param.6) | copy-start | bytes 3932164
  3.4 1.2 copy-start.2
  3.5 1.9 %copy-start = (s32[1,1024]{1,0:T(1,128)S(1)}, s32[1,1024]{1,0:T(1,128)}, u32[]{:S(2)}) copy-start(s32[1,1024]{1,0:T(1,128)} %row_ref.1) | copy-start | bytes 12292
  3.5 1.9 %copy-start.3 = (s32[1,128]{1,0:T(1,128)S(1)}, s32[1,128]{1,0:T(1,128)}, u32[]{:S(2)}) copy-start(s32[1,128]{1,0:T(1,128)} %param.8) | copy-start | bytes 1540
